TPU v7x, 32 devices: a whole 2x2x4 slice. The times are simulated.
32 devices in a mesh: groups: 2 (over x), sensor: 16 (over z, y, core).
Axes of the slice: x: 2, y: 2, z: 4, core: 2. Of those that a mesh axis runs over, the one named last changes fastest.
Arguments:
- series: float32 [288, 1536], P(None, ('groups', 'sensor')), parts along dimension 1, may hold values from -6 to 6
- starts: int32 [2], P('groups'), parts along dimension 0, may hold values from 0 to 276
- sensor_order: int32 [1536], P(('groups', 'sensor')), parts along dimension 0, may hold values from 0 to 767, each once
- emb_src: float32 [10, 1536], P(None, ('groups', 'sensor')), parts along dimension 1, may hold values from -4.4 to 330
- emb_dst: float32 [10, 1536], P(None, ('groups', 'sensor')), parts along dimension 1, may hold values from -4.4 to 4.4
- start_proj: float32 [2, 32], replicated, may hold values from -4 to 4
- conv_weight: bfloat16 [64, 64], replicated, may hold values from -0.75 to 0.75
- mix_weight: bfloat16 [96, 32], replicated, may hold values from -0.625 to 0.625
- out_grad: bfloat16 [1536, 384], P(('groups', 'sensor')), parts along dimension 0, may hold values from -0.59765625 to 0.59765625
Outputs:
- layer_out: bfloat16 [1536, 384], P(('groups', 'sensor')), parts along dimension 0
- grad_src: float32 [10, 1536], P(None, ('groups', 'sensor')), parts along dimension 1
- grad_dst: float32 [10, 1536], P(None, ('groups', 'sensor')), parts along dimension 1
- grad_mix: float32 [192, 32], P('groups'), parts along dimension 0
There are 2 independent parts, one for each index of `groups`. A program takes and returns all parts, laid end to end along the dimension named above; an argument that names none is the same for every part. Nothing has to cross between parts.
All inputs are finite; a program needn't handle non-finite values.
Results may differ from a plain program's by a relative error of at most 0.035.
Values may be sent and summed in bfloat16 or wider, within the bound.
A program may use at most 64 MiB of HBM per device.

v0:
```python
import math
import jax
import jax.numpy as jnp
from jax import lax
from jax.sharding import PartitionSpec as P

STEPS = 12
highest = lax.Precision.HIGHEST


def front(readings, start_proj, conv_weight):
    sensors_here = readings.shape[0]
    channels = start_proj.shape[1]
    padded = jnp.concatenate(
        [jnp.zeros(readings.shape[:-1] + (1,), jnp.float32), readings], axis=-1
    )
    inputs = (padded[..., None] * start_proj[0] + start_proj[1]).astype(jnp.bfloat16)
    paired = jnp.concatenate([inputs[:, :, :-1, :], inputs[:, :, 1:, :]], axis=-1).reshape(
        -1, 2 * channels
    )
    gate_terms = jnp.dot(paired, conv_weight, preferred_element_type=jnp.float32)
    hidden = (jnp.tanh(gate_terms[:, :channels]) * jax.nn.sigmoid(gate_terms[:, channels:])).astype(
        jnp.bfloat16
    )
    return (hidden.reshape(sensors_here, -1), inputs[:, :, 1:, :].reshape(sensors_here, -1))


def mixing(residual, hidden, diffused, second, mix_weight):
    channels = mix_weight.shape[1]
    stacked = jnp.concatenate(
        [member.reshape(-1, channels) for member in (hidden, diffused, second)], axis=1
    )
    summed = residual.reshape(-1, channels).astype(jnp.float32) + jnp.dot(
        stacked, mix_weight, preferred_element_type=jnp.float32
    )
    return (summed.astype(jnp.bfloat16).reshape(hidden.shape[0], -1), stacked)


def channel_grads(out_grad, mix_weight):
    channels = mix_weight.shape[1]
    row_count = out_grad.shape[0]
    flat_grad = out_grad.reshape(-1, channels)
    dims = (((1,), (1,)), ((), ()))
    grad_once = lax.dot_general(
        flat_grad, mix_weight[channels : 2 * channels], dims, preferred_element_type=jnp.float32
    )
    grad_twice = lax.dot_general(
        flat_grad, mix_weight[2 * channels :], dims, preferred_element_type=jnp.float32
    )
    return (
        grad_once.astype(jnp.bfloat16).reshape(row_count, -1),
        grad_twice.astype(jnp.bfloat16).reshape(row_count, -1),
    )


def tile_probs(rows_emb, cols_emb, row_max, row_total):
    scores = jnp.einsum("ei,ej->ij", rows_emb, cols_emb, precision=highest)
    shares = jnp.exp(jnp.maximum(scores, 0.0) - row_max[:, None]) / row_total[:, None]
    return (scores, shares)


def pair_dot(left, right):
    return lax.dot_general(
        left, right, (((1,), (1,)), ((), ())), preferred_element_type=jnp.float32
    )


def in_blocks(step_fn, status, members, axis_dim):
    amount = members[0].shape[axis_dim]
    span_size = math.gcd(amount, 512)

    def advance(position, current):
        opening = position * span_size
        sliced = tuple(
            (lax.dynamic_slice_in_dim(member, opening, span_size, axis_dim) for member in members)
        )
        return step_fn(current, sliced, opening)

    return lax.fori_loop(0, amount // span_size, advance, status)


def score_grads(status, emb_src, cols_dst, offset, scores, shares, dweights):
    grad_rows, grad_cols = status
    dscore = jnp.where(scores > 0.0, shares * dweights, 0.0)
    grad_rows = grad_rows + jnp.einsum("ej,ij->ei", cols_dst, dscore, precision=highest)
    span_size = dscore.shape[1]
    current = lax.dynamic_slice_in_dim(grad_cols, offset, span_size, 1)
    added = current + jnp.einsum("ei,ij->ej", emb_src, dscore, precision=highest)
    return (grad_rows, lax.dynamic_update_slice_in_dim(grad_cols, added, offset, 1))


def per_device(
    series, starts, sensor_order, emb_src, emb_dst, start_proj, conv_weight, mix_weight, out_grad
):
    local_rows = sensor_order.shape[0]
    embed_dim = emb_src.shape[0]
    channels = start_proj.shape[1]
    all_rows = local_rows * lax.axis_size("sensor")
    windows = jax.vmap(lambda first_step: lax.dynamic_slice_in_dim(series, first_step, STEPS, 0))(
        starts
    )
    flat_windows = windows.reshape(-1, local_rows)
    window_rows = flat_windows.shape[0]

    def pick_step(status, members, offset):
        readings_sum, dst_all = status
        block_windows, block_dst = members
        span_size = block_windows.shape[1]
        onehot = (sensor_order[:, None] == offset + lax.iota(jnp.int32, span_size)[None, :]).astype(
            jnp.float32
        )
        readings_sum = readings_sum + jnp.einsum(
            "wj,pj->wp", block_windows, onehot, precision=highest
        )
        return (readings_sum, lax.dynamic_update_slice_in_dim(dst_all, block_dst, offset, 1))

    readings_sum, dst_all = in_blocks(
        pick_step,
        (
            jnp.zeros((window_rows, local_rows), jnp.float32),
            jnp.zeros((embed_dim, all_rows), jnp.float32),
        ),
        (
            lax.all_gather(flat_windows, "sensor", axis=1, tiled=True),
            lax.all_gather(emb_dst, "sensor", axis=1, tiled=True),
        ),
        1,
    )
    readings = readings_sum.T.reshape(local_rows, -1, STEPS)
    hidden, residual = front(readings, start_proj, conv_weight)
    feat_cols = hidden.shape[1]
    span_all = math.gcd(all_rows, 512)

    def stat_step(position, current):
        best_score, summed = current
        cols_dst = lax.dynamic_slice_in_dim(dst_all, position * span_all, span_all, 1)
        scores = jnp.maximum(jnp.einsum("ei,ej->ij", emb_src, cols_dst, precision=highest), 0.0)
        new_best = jnp.maximum(best_score, jnp.max(scores, axis=1))
        summed = summed * jnp.exp(best_score - new_best) + jnp.sum(
            jnp.exp(scores - new_best[:, None]), axis=1
        )
        return (new_best, summed)

    row_max, row_total = lax.fori_loop(
        0,
        all_rows // span_all,
        stat_step,
        (jnp.zeros((local_rows,), jnp.float32), jnp.zeros((local_rows,), jnp.float32)),
    )
    grad_once, grad_twice = channel_grads(out_grad, mix_weight)

    def spread_step(status, members, offset):
        block_feat = members[0]
        cols_dst = lax.dynamic_slice_in_dim(dst_all, offset, block_feat.shape[0], 1)
        scores, shares = tile_probs(emb_src, cols_dst, row_max, row_total)
        return status + jnp.dot(
            shares.astype(jnp.bfloat16), block_feat, preferred_element_type=jnp.float32
        )

    first_init = jnp.zeros((local_rows, feat_cols), jnp.float32)
    first_result = in_blocks(
        spread_step, first_init, (lax.all_gather(hidden, "sensor", axis=0, tiled=True),), 0
    )
    diffused = first_result.astype(jnp.bfloat16)

    def plain_step(status, members, offset):
        accumulated, grad_rows, grad_cols = status
        return (spread_step(accumulated, members, offset), grad_rows, grad_cols)

    second_init = (
        jnp.zeros((local_rows, feat_cols), jnp.float32),
        jnp.zeros((embed_dim, local_rows), jnp.float32),
        jnp.zeros((embed_dim, all_rows), jnp.float32),
    )
    second_result = in_blocks(
        plain_step, second_init, (lax.all_gather(diffused, "sensor", axis=0, tiled=True),), 0
    )
    second_full, grad_rows, grad_cols = second_result
    second = second_full.astype(jnp.bfloat16)
    layer_out, stacked = mixing(residual, hidden, diffused, second, mix_weight)
    mix_part = lax.dot_general(
        stacked,
        out_grad.reshape(-1, channels),
        (((0,), (0,)), ((), ())),
        preferred_element_type=jnp.float32,
    )
    span_size = math.gcd(lax.axis_size("sensor") * local_rows, 512)

    def piece_term(position):
        cols_dst = lax.dynamic_slice_in_dim(dst_all, position * span_size, span_size, 1)
        scores, shares = tile_probs(emb_src, cols_dst, row_max, row_total)
        return lax.dot_general(
            shares.astype(jnp.bfloat16),
            grad_twice,
            (((0,), (0,)), ((), ())),
            preferred_element_type=jnp.float32,
        )

    adjoint_sum = lax.psum_scatter(
        lax.map(
            piece_term,
            jnp.arange(lax.axis_size("sensor") * local_rows // span_size, dtype=jnp.int32),
        ).reshape(lax.axis_size("sensor") * local_rows, -1),
        "sensor",
        scatter_dimension=0,
        tiled=True,
    )
    carried = (grad_once.astype(jnp.float32) + adjoint_sum).astype(jnp.bfloat16)
    row_delta = jnp.sum(
        grad_twice.astype(jnp.float32) * second_full + carried.astype(jnp.float32) * first_result,
        axis=1,
    )

    def pair_step(status, members, offset):
        block_hidden, block_diff = members
        cols_dst = lax.dynamic_slice_in_dim(dst_all, offset, block_hidden.shape[0], 1)
        scores, shares = tile_probs(emb_src, cols_dst, row_max, row_total)
        dweights = (
            pair_dot(grad_twice, block_diff) + pair_dot(carried, block_hidden) - row_delta[:, None]
        )
        return score_grads(status, emb_src, cols_dst, offset, scores, shares, dweights)

    grad_rows, grad_cols = in_blocks(
        pair_step,
        (grad_rows, grad_cols),
        (
            lax.all_gather(hidden, "sensor", axis=0, tiled=True),
            lax.all_gather(diffused, "sensor", axis=0, tiled=True),
        ),
        0,
    )
    grad_dst = lax.psum_scatter(grad_cols, "sensor", scatter_dimension=1, tiled=True)
    grad_mix = lax.psum(mix_part, "sensor")
    return (layer_out, grad_rows, grad_dst, grad_mix)


def solution(mesh):
    placed = (
        P(None, ("groups", "sensor")),
        P("groups"),
        P(("groups", "sensor")),
        P(None, ("groups", "sensor")),
        P(None, ("groups", "sensor")),
        P(),
        P(),
        P(),
        P(("groups", "sensor"), None),
    )
    return jax.shard_map(
        per_device,
        mesh=mesh,
        in_specs=placed,
        out_specs=(
            P(("groups", "sensor"), None),
            P(None, ("groups", "sensor")),
            P(None, ("groups", "sensor")),
            P("groups", None),
        ),
        check_vma=False,
    )
```

profile of v0, /device:TPU:0, one launch (start us, length us, event | category | flops | bytes accessed | tf_op | source)
XLA Modules:
  0.0 194.4 jit_solution(2964574075094498716)
XLA Ops:
  8.2 23.4 %all-gather = f32[16,48,12]{1,2,0:T(8,128)S(1)} all-gather(f32[1,48,12]{1,2,0:T(8,128)S(1)} %bitcast.98), channel_id=1, replica_groups=mesh['groups'=2,'sensor'=16] {'sensor'}, dimensions={0}, use_global_device_ids=true | all-gather | bytes 39168 | tf_op jit(solution)/shard_map/all_gather | solution.py:124
  31.8 18.0 %all-gather.1 = f32[16,48,10]{1,2,0:T(8,128)S(1)} all-gather(f32[1,48,10]{1,2,0:T(8,128)} %bitcast.100), channel_id=1, replica_groups=mesh['groups'=2,'sensor'=16] {'sensor'}, dimensions={0}, use_global_device_ids=true | all-gather | bytes 32640 | tf_op jit(solution)/shard_map/all_gather | solution.py:125
  50.0 2.7 %while.88 = (s32[]{:T(128)}, f32[12,48]{1,0:T(8,128)S(1)}, f32[10,768]{1,0:T(8,128)S(1)}, f32[12,768]{1,0:T(8,128)S(1)}, s32[48]{0:T(128)}, /*index=5*/f32[10,76...) while((s32[]{:T(128)}, f32[12,48]{1,0:T(8,128)S(1)}, f32[10,768]{1,0:T(8,128)S(1)}, ...), condition=%wide.region_1.0_spmd.clone, body=%wide.region_0.0_spmd.clone.sunk | while | flops 1783175 | bytes 62065 | solution.py:79
  50.0 0.8 convolution_add_fusion.10
  50.9 0.8 convolution_add_fusion.10
  51.9 0.8 convolution_add_fusion.10
  52.7 1.8 while.89
  52.8 0.3 fusion.128
  53.4 0.3 fusion.128
  53.9 0.3 fusion.128
  54.7 0.3 convolution_convert_fusion.1
  55.3 7.5 %while.87 = (s32[]{:T(128)}, f32[3,256,384]{2,1,0:T(8,128)}, s32[3]{0:T(128)S(1)}, f32[10,768]{1,0:T(8,128)S(1)}, f32[10,48]{1,0:T(8,128)S(1)}, /*index=5*/f32[4...) while((s32[]{:T(128)}, f32[3,256,384]{2,1,0:T(8,128)}, ...), condition=%wide.region_11.12_spmd, body=%wide.region_10.11_spmd.sunk | while | flops 10960902 | bytes 505023 | solution.py:200
  55.3 0.6 dynamic_slice.136
  56.8 1.0 fusion.124
  57.8 0.6 dynamic_slice.136
  59.3 1.0 fusion.124
  60.3 0.6 dynamic_slice.136
  61.5 0.3 fusion.123
  61.8 1.0 fusion.124
  62.9 0.6 copy-done.6
  64.2 0.3 copy-done.5
  65.1 20.4 %all_gather.16 = bf16[768,384]{1,0:T(8,128)(2,1)S(1)} all-gather(bf16[48,384]{1,0:T(8,128)(2,1)S(1)} %reshape.86), channel_id=1, replica_groups=mesh['groups'=2,'sensor'=16] {'sensor'}, dimensions={0}, use_global_device_ids=true | all-gather | bytes 626688 | tf_op jit(solution)/shard_map/all_gather | solution.py:162
  85.5 1.4 while.90
  87.7 20.1 %all_gather.17 = bf16[768,384]{1,0:T(8,128)(2,1)S(1)} all-gather(bf16[48,384]{1,0:T(8,128)(2,1)S(1)} %convert_element_type.68), channel_id=1, replica_groups=mesh['groups'=2,'sensor'=16] {'sensor'}, dimensions={0}, use_global_device_ids=true | all-gather | bytes 626688 | tf_op jit(solution)/shard_map/all_gather | solution.py:176
  107.9 1.4 while.91
  109.2 12.6 %reduce-scatter.5.cloned.1.call-done = f32[48,384]{1,0:T(8,128)} async-done(((f32[768,384]{1,0:T(8,128)}), f32[48,384]{1,0:T(8,128)}) %reduce-scatter.5.cloned.1.call-update) | async-done | bytes 73744 | tf_op jit(solution)/shard_map/reduce_scatter | solution.py:199
  121.9 1.0 add_reduce_fusion
  123.2 3.0 %while.92 = (s32[]{:T(128)}, f32[10,48]{1,0:T(8,128)S(1)}, f32[10,768]{1,0:T(8,128)S(1)}, f32[10,768]{1,0:T(8,128)S(1)}, f32[10,48]{1,0:T(8,128)S(1)}, /*index=5...) while((s32[]{:T(128)}, f32[10,48]{1,0:T(8,128)S(1)}, ...), condition=%wide.region_15.16_spmd.clone, body=%wide.region_14.15_spmd.clone.sunk | while | flops 23399876 | bytes 904809 | solution.py:79
  126.2 0.9 copy.46
  127.7 0.8 reshape.89
  128.5 57.7 %psum.7 = f32[96,32]{0,1:T(8,128)} all-reduce(f32[96,32]{0,1:T(8,128)S(1)} %fusion.55), channel_id=1, replica_groups=mesh['groups'=2,'sensor'=16] {'sensor'}, use_global_device_ids=true, to_apply=%region_17.18 | all-reduce | flops 3072 | bytes 24576 | tf_op jit(solution)/shard_map/psum | solution.py:233
  186.1 1.4 copy.47
  (107 shorter events, 10.7 us)
Async XLA Ops:
  7.2 0.9 copy-start
  7.2 45.6 %copy-start.1 = (f32[10,48]{1,0:T(8,128)S(1)}, f32[10,48]{1,0:T(8,128)}, u32[]{:S(2)}) copy-start(f32[10,48]{1,0:T(8,128)} %param.24) | copy-start | bytes 5764
  7.2 114.7 %reduce-scatter.5.cloned.1.call-start = ((), (), s32[]{:S(2)}) async-start(), calls=%async_computation.2 | async-start | bytes 1253376 | tf_op jit(solution)/shard_map/reduce_scatter | solution.py:199
  31.7 22.8 %copy-start.3 = (bf16[48,384]{1,0:T(8,128)(2,1)S(1)}, bf16[48,384]{1,0:T(8,128)(2,1)}, u32[]{:S(2)}) copy-start(bf16[48,384]{1,0:T(8,128)(2,1)} %param.29) | copy-start | bytes 110596
  31.8 22.9 %copy-start.4 = (bf16[96,32]{0,1:T(8,128)(2,1)S(1)}, bf16[96,32]{0,1:T(8,128)(2,1)}, u32[]{:S(2)}) copy-start(bf16[96,32]{0,1:T(8,128)(2,1)} %param.28) | copy-start | bytes 18436
  62.8 0.7 copy-start.6
  62.8 123.3 %reduce-scatter.7.cloned.1.call-start = ((), (), s32[]{:S(2)}) async-start(), calls=%async_computation.3 | async-start | bytes 417792
  63.8 0.7 copy-start.5
  126.2 61.3 %copy-start.2 = (f32[10,48]{1,0:T(8,128)}, f32[10,48]{1,0:T(8,128)S(1)}, u32[]{:S(2)}) copy-start(f32[10,48]{1,0:T(8,128)S(1)} %get-tuple-element.696) | copy-start | bytes 5764
Sparse Core Ops, SparseCore 0:
  62.9 58.8 reduce-scatter.4
  127.3 54.7 reduce-scatter.6
where the time goes:
time: 195 us; the launch traced here: 194 us
  blocking collectives  140 us (72%)
  between operations  15 us (8%)
  matrix products  13.9 us (7%)
  waiting for transfers between devices  12.7 us (7%)
  local copies, waits for them, and re-layouts  8.47 us (4%)
  loops' own time  2.58 us (1%)
  other arithmetic  2.1 us (1%)
    psum x1, blocking collectives, per_device(): grad_mix = lax.psum(mix_part, 'sensor')  57.7 us
    all_gather x1, blocking collectives, per_device(): lax.all_gather(flat_windows, 'sensor', axis=1, tiled=True)  23.4 us
    all_gather x1, blocking collectives, per_device(): lax.all_gather(hidden, 'sensor', axis=0, tiled=True)  20.4 us
    all_gather x1, blocking collectives, per_device(): lax.all_gather(diffused, 'sensor', axis=0, tiled=True)  20.1 us
    all_gather x1, blocking collectives, per_device(): lax.all_gather(emb_dst, 'sensor', axis=1, tiled=True)  18 us
    reduce_scatter x1, waiting for transfers between devices, per_device(): lax.psum_scatter(lax.map(piece_term, jnp.arange(lax.axis_size('sensor') *...  12.6 us
  transfers between devices with their start and end apart: 2, of which 1 were waited for; matrix products, arithmetic and copies ran while one was open for 3% of the time, Pallas kernels for 0%

commit v1 on v0

--- a/solution.py
+++ b/solution.py
@@ -6,6 +6,18 @@
 
 STEPS = 12
 highest = lax.Precision.HIGHEST
+
+
+def gather_by_bits(x, axis, dim):
+    ways, here = (lax.axis_size(axis), lax.axis_index(axis))
+    grown, reach = (x, 1)
+    while reach < ways:
+        theirs = lax.ppermute(grown, axis, [(d, d ^ reach) for d in range(ways)])
+        mine_first = jnp.concatenate([grown, theirs], axis=dim)
+        theirs_first = jnp.concatenate([theirs, grown], axis=dim)
+        grown = jnp.where(here & reach == 0, mine_first, theirs_first)
+        reach = 2 * reach
+    return grown
 
 
 def front(readings, start_proj, conv_weight):
@@ -172,9 +184,7 @@
         jnp.zeros((embed_dim, local_rows), jnp.float32),
         jnp.zeros((embed_dim, all_rows), jnp.float32),
     )
-    second_result = in_blocks(
-        plain_step, second_init, (lax.all_gather(diffused, "sensor", axis=0, tiled=True),), 0
-    )
+    second_result = in_blocks(plain_step, second_init, (gather_by_bits(diffused, "sensor", 0),), 0)
     second_full, grad_rows, grad_cols = second_result
     second = second_full.astype(jnp.bfloat16)
     layer_out, stacked = mixing(residual, hidden, diffused, second, mix_weight)

time: 195 us -> 221 us (1.13)
  waiting for transfers between devices: 12.7 us -> 35 us
  blocking collectives: 140 us -> 143 us
    reduce_scatter x1, waiting for transfers between devices: 12.6 us -> 30.6 us  [per_device(): lax.psum_scatter(lax.map(piece_term, jnp.arange(lax.axis_size('sensor') *...]
    ppermute x0 -> x4, waiting for transfers between devices: none -> 4.3 us  [gather_by_bits(): theirs = lax.ppermute(grown, axis, [(d, d ^ reach) for d in range(ways)])]
    all_gather x1, blocking collectives: 20.1 us -> 23.2 us  [per_device(): lax.all_gather(diffused, 'sensor', axis=0, tiled=True)]
  transfers between devices with their start and end apart: 2 -> 6, of which waited for: 1 -> 3; matrix products, arithmetic and copies ran while one was open for 3% -> 5% of each run, Pallas kernels for 0% -> 0%
where the time goes in v1:
time: 221 us
  blocking collectives  143 us (65%)
  waiting for transfers between devices  35 us (16%)
  between operations  15.1 us (7%)
  matrix products  13.8 us (6%)
  local copies, waits for them, and re-layouts  8.2 us (4%)
  loops' own time  2.6 us (1%)
  other arithmetic  2.43 us (1%)
    psum x1, blocking collectives, per_device(): grad_mix = lax.psum(mix_part, 'sensor')  57.8 us
    reduce_scatter x1, waiting for transfers between devices, per_device(): lax.psum_scatter(lax.map(piece_term, jnp.arange(lax.axis_size('sensor') *...  30.6 us
    all_gather x1, blocking collectives, per_device(): lax.all_gather(flat_windows, 'sensor', axis=1, tiled=True)  23.4 us
    all_gather x1, blocking collectives, per_device(): lax.all_gather(diffused, 'sensor', axis=0, tiled=True)  23.2 us
    all_gather x1, blocking collectives, per_device(): lax.all_gather(hidden, 'sensor', axis=0, tiled=True)  20.4 us
    all_gather x1, blocking collectives, per_device(): lax.all_gather(emb_dst, 'sensor', axis=1, tiled=True)  18 us
  transfers between devices with their start and end apart: 6, of which 3 were waited for; matrix products, arithmetic and copies ran while one was open for 5% of the time, Pallas kernels for 0%

profile of v1, /device:TPU:0, one launch (start us, length us, event | category | flops | bytes accessed | tf_op | source)
XLA Modules:
  0.0 221.0 jit_solution(16845264735012282721)
XLA Ops:
  7.3 0.8 slice_bitcast_fusion.1
  8.8 23.4 %all-gather = f32[16,48,12]{1,2,0:T(8,128)S(1)} all-gather(f32[1,48,12]{1,2,0:T(8,128)S(1)} %bitcast.98), channel_id=1, replica_groups=mesh['groups'=2,'sensor'=16] {'sensor'}, dimensions={0}, use_global_device_ids=true | all-gather | bytes 39168 | tf_op jit(solution)/shard_map/all_gather | solution.py:136
  32.4 18.0 %all-gather.1 = f32[16,48,10]{1,2,0:T(8,128)S(1)} all-gather(f32[1,48,10]{1,2,0:T(8,128)} %bitcast.100), channel_id=1, replica_groups=mesh['groups'=2,'sensor'=16] {'sensor'}, dimensions={0}, use_global_device_ids=true | all-gather | bytes 32640 | tf_op jit(solution)/shard_map/all_gather | solution.py:137
  50.6 2.7 %while.88 = (s32[]{:T(128)}, f32[12,48]{1,0:T(8,128)S(1)}, f32[10,768]{1,0:T(8,128)S(1)}, f32[12,768]{1,0:T(8,128)S(1)}, s32[48]{0:T(128)}, /*index=5*/f32[10,76...) while((s32[]{:T(128)}, f32[12,48]{1,0:T(8,128)S(1)}, f32[10,768]{1,0:T(8,128)S(1)}, ...), condition=%wide.region_1.0_spmd.clone, body=%wide.region_0.0_spmd.clone.sunk | while | flops 1783175 | bytes 62065 | solution.py:91
  50.7 0.8 convolution_add_fusion.10
  51.6 0.8 convolution_add_fusion.10
  52.5 0.8 convolution_add_fusion.10
  53.8 1.8 while.89
  53.8 0.3 fusion.128
  54.4 0.3 fusion.128
  56.3 20.4 %all_gather.15 = bf16[768,384]{1,0:T(8,128)(2,1)S(1)} all-gather(bf16[48,384]{1,0:T(8,128)(2,1)S(1)} %reshape.86), channel_id=1, replica_groups=mesh['groups'=2,'sensor'=16] {'sensor'}, dimensions={0}, use_global_device_ids=true | all-gather | bytes 626688 | tf_op jit(solution)/shard_map/all_gather | solution.py:174
  76.7 1.4 while.90
  78.1 0.4 collective-permute-start
  78.7 0.7 collective-permute-done
  79.4 0.4 collective-permute-start.1
  80.4 3.6 %collective-permute-done.1 = bf16[96,384]{1,0:T(8,128)(2,1)S(1)} collective-permute-done((bf16[96,384]{1,0:T(8,128)(2,1)S(1)}, bf16[96,384]{1,0:T(8,128)(2,1)S(1)}, u32[]{:S(2)}, u32[]{:S(2)}) %collective-permute-start.1) | collective-permute-done | bytes 73760 | tf_op jit(solution)/shard_map/ppermute | solution.py:15
  84.1 7.5 %while.87 = (s32[]{:T(128)}, f32[3,256,384]{2,1,0:T(8,128)}, s32[3]{0:T(128)S(1)}, f32[10,768]{1,0:T(8,128)S(1)}, f32[10,48]{1,0:T(8,128)S(1)}, /*index=5*/f32[4...) while((s32[]{:T(128)}, f32[3,256,384]{2,1,0:T(8,128)}, ...), condition=%wide.region_11.12_spmd, body=%wide.region_10.11_spmd.sunk | while | flops 10960902 | bytes 505023 | solution.py:210
  84.1 0.6 dynamic_slice.136
  85.6 1.0 fusion.124
  86.6 0.6 dynamic_slice.136
  88.1 1.0 fusion.124
  89.1 0.6 dynamic_slice.136
  90.6 1.0 fusion.124
  92.9 23.2 %all_gather.16 = bf16[768,384]{1,0:T(8,128)(2,1)S(1)} all-gather(bf16[48,384]{1,0:T(8,128)(2,1)S(1)} %convert_element_type.68), channel_id=1, replica_groups=mesh['groups'=2,'sensor'=16] {'sensor'}, dimensions={0}, use_global_device_ids=true | all-gather | bytes 626688 | tf_op jit(solution)/shard_map/all_gather | solution.py:238
  116.4 1.4 while.91
  117.8 30.6 %reduce-scatter.5.cloned.1.call-done = f32[48,384]{1,0:T(8,128)} async-done(((f32[768,384]{1,0:T(8,128)}), f32[48,384]{1,0:T(8,128)}) %reduce-scatter.5.cloned.1.call-update) | async-done | bytes 73744 | tf_op jit(solution)/shard_map/reduce_scatter | solution.py:209
  148.4 1.0 add_reduce_fusion
  149.7 3.0 %while.92 = (s32[]{:T(128)}, f32[10,48]{1,0:T(8,128)S(1)}, f32[10,768]{1,0:T(8,128)S(1)}, f32[10,768]{1,0:T(8,128)S(1)}, f32[10,48]{1,0:T(8,128)S(1)}, /*index=5...) while((s32[]{:T(128)}, f32[10,48]{1,0:T(8,128)S(1)}, ...), condition=%wide.region_15.16_spmd.clone, body=%wide.region_14.15_spmd.clone.sunk | while | flops 23399876 | bytes 904809 | solution.py:91
  152.7 0.9 copy.46
  154.2 0.8 reshape.89
  155.0 57.8 %psum.7 = f32[96,32]{0,1:T(8,128)} all-reduce(f32[96,32]{0,1:T(8,128)S(1)} %fusion.55), channel_id=1, replica_groups=mesh['groups'=2,'sensor'=16] {'sensor'}, use_global_device_ids=true, to_apply=%region_17.18 | all-reduce | flops 3072 | bytes 24576 | tf_op jit(solution)/shard_map/psum | solution.py:243
  212.8 1.4 copy.47
  (117 shorter events, 11.9 us)
Async XLA Ops:
  7.2 1.5 copy-start
  7.2 141.2 %reduce-scatter.5.cloned.1.call-start = ((), (), s32[]{:S(2)}) async-start(), calls=%async_computation.2 | async-start | bytes 1253376 | tf_op jit(solution)/shard_map/reduce_scatter | solution.py:209
  50.5 3.3 %copy-start.1 = (f32[10,48]{1,0:T(8,128)S(1)}, f32[10,48]{1,0:T(8,128)}, u32[]{:S(2)}) copy-start(f32[10,48]{1,0:T(8,128)} %param.24) | copy-start | bytes 5764
  53.7 2.0 copy-start.5
  76.7 1.8 copy-start.3
  76.7 3.1 %copy-start.4 = (bf16[96,32]{0,1:T(8,128)(2,1)S(1)}, bf16[96,32]{0,1:T(8,128)(2,1)}, u32[]{:S(2)}) copy-start(bf16[96,32]{0,1:T(8,128)(2,1)} %param.28) | copy-start | bytes 18436
  78.1 1.3 collective-permute-start
  79.4 4.6 %collective-permute-start.1 = (bf16[96,384]{1,0:T(8,128)(2,1)S(1)}, bf16[96,384]{1,0:T(8,128)(2,1)S(1)}, u32[]{:S(2)}, u32[]{:S(2)}) collective-permute-start(bf16[96,384]{1,0:T(8,128)(2,1)S(1)} %maximum_select_fusion.3), channel_id=1, source_target_pairs={{0,2},{1,3},{2,0},{3,1},{4,6},{5,7},{6,4},{7,5},{8,10},{9,11},{10,... | collective-permute-start | bytes 221192 | tf_op jit(solution)/shard_map/ppermute | solution.py:15
  84.0 7.7 %collective-permute-start.2 = (bf16[192,384]{1,0:T(8,128)(2,1)S(1)}, bf16[192,384]{1,0:T(8,128)(2,1)S(1)}, u32[]{:S(2)}, u32[]{:S(2)}) collective-permute-start(bf16[192,384]{1,0:T(8,128)(2,1)S(1)} %maximum_select_fusion.2), channel_id=1, source_target_pairs={{0,4},{1,5},{2,6},{3,7},{4,0},{5,1},{6,2},{7,3},{8,12},{9,13},{10,... | collective-permute-start | bytes 442376 | tf_op jit(solution)/shard_map/ppermute | solution.py:15
  91.6 121.1 %reduce-scatter.7.cloned.1.call-start = ((), (), s32[]{:S(2)}) async-start(), calls=%async_computation.3 | async-start | bytes 417792
  91.8 24.4 %collective-permute-start.3 = (bf16[384,384]{1,0:T(8,128)(2,1)S(1)}, bf16[384,384]{1,0:T(8,128)(2,1)S(1)}, u32[]{:S(2)}, u32[]{:S(2)}) collective-permute-start(bf16[384,384]{1,0:T(8,128)(2,1)S(1)} %maximum_select_fusion.1), channel_id=1, source_target_pairs={{0,8},{1,9},{2,10},{3,11},{4,12},{5,13},{6,14},{7,15},{8,0},{9,1},... | collective-permute-start | bytes 884744 | tf_op jit(solution)/shard_map/ppermute | solution.py:15
  152.7 61.5 %copy-start.2 = (f32[10,48]{1,0:T(8,128)}, f32[10,48]{1,0:T(8,128)S(1)}, u32[]{:S(2)}) copy-start(f32[10,48]{1,0:T(8,128)S(1)} %get-tuple-element.696) | copy-start | bytes 5764
Sparse Core Ops, SparseCore 0:
  91.8 56.6 reduce-scatter.4
  153.8 54.7 reduce-scatter.6
